TPU v7x, 32 devices: a whole 2x2x4 slice. The times are simulated.
32 devices in a mesh: dp: 8 (over z, x), mp: 4 (over y, core).
Axes of the slice: x: 2, y: 2, z: 4, core: 2. Of those that a mesh axis runs over, the one named last changes fastest.
Arguments:
- tokens: bfloat16 [256, 48, 3584], P('dp', None, 'mp'), may hold values from -180 to 180
- norm_gain: float32 [3584], replicated, may hold values from 0.1 to 1.9
- w_query: bfloat16 [3584, 3584], P('dp', 'mp'), may hold values from -0.16 to 0.16
- w_keyval: bfloat16 [3584, 2, 512], P('dp', None, 'mp'), may hold values from -0.16 to 0.16
- w_out: bfloat16 [3584, 3584], P('mp', 'dp'), may hold values from -0.09375 to 0.09375
- residents: bfloat16 [8, 2048, 3584], P('dp', 'mp'), may hold values from -6 to 6
- lengths: int32 [256], P('dp'), may hold values from 6 to 48
- cluster: int32 [256, 1], P('dp'), may hold values from 0 to 7; in each aligned block of 32 rows (0 to 31, 32 to 63, ...) at most 4 rows name the same one
- owner: int32 [8], replicated, may hold values from 0 to 7, each once
- counts: int32 [8], replicated, may hold values from 256 to 2048
- flags: int32 [256], P('dp'), may hold values 0 or 1
Outputs:
- similarity: float32 [256, 2048], P('dp', 'mp')
Inputs may be any that keep to these rules, and one draw needn't show every extreme that they name: Each dialogue's cluster; among the 32 dialogues of one index of dp (aligned blocks of rows) no cluster is named more than 4 times. owner gives every cluster a distinct index of dp that holds its residents.
All inputs are finite; a program needn't handle non-finite values. No bound on the sum of `flags` on one device may be relied on, other than what follows from the above.
Results may differ from a plain program's by a relative error of at most 0.013.
Values may be sent and summed in bfloat16 or wider, within the bound.
A program may use at most 128 MiB of HBM per device.

v0:
```python
import math
import jax
import jax.numpy as jnp
from jax import lax
from jax.sharding import PartitionSpec as P

HEAD_DIM = 128
rope_base = 1000000.0
logit_scale = 100.0


def rotate(values, positions):
    half = values.shape[-1] // 2
    freqs = rope_base ** (-jnp.arange(half, dtype=jnp.float32) * 2.0 / values.shape[-1])
    angles = positions.astype(jnp.float32)[:, None] * freqs[None, :]
    cosine = jnp.cos(angles)[:, None, :]
    sine = jnp.sin(angles)[:, None, :]
    first = values[..., :half]
    second = values[..., half:]
    return jnp.concatenate(
        [first * cosine - second * sine, second * cosine + first * sine], axis=-1
    )


def attend(query, keys, values, length):
    seq_len = query.shape[0]
    kv_count = keys.shape[1]
    group = query.shape[1] // kv_count
    grouped = query.reshape(seq_len, kv_count, group, query.shape[-1])
    scores = jnp.einsum(
        "qkgd,pkd->kgqp", grouped, keys, preferred_element_type=jnp.float32
    ) / math.sqrt(query.shape[-1])
    row_pos = jnp.arange(seq_len)[:, None]
    col_pos = jnp.arange(seq_len)[None, :]
    allowed = (col_pos <= row_pos) & (col_pos < length)
    scores = jnp.where(allowed, scores, -1e30)
    highest = jnp.max(scores, axis=-1, keepdims=True)
    expanded = jnp.exp(scores - highest)
    weights = (expanded / jnp.sum(expanded, axis=-1, keepdims=True)).astype(jnp.bfloat16)
    context = jnp.einsum("kgqp,pkd->qkgd", weights, values, preferred_element_type=jnp.float32)
    valid = (jnp.arange(seq_len) < length).astype(jnp.float32)
    pooled = jnp.sum(context * valid[:, None, None, None], axis=0) / length.astype(jnp.float32)
    return pooled.reshape(-1)


def local(
    tokens, norm_gain, w_query, w_keyval, w_out, residents, lengths, cluster, owner, counts, flags
):
    gathered = lax.all_gather(tokens, "mp", axis=2, tiled=True)
    dialogs, seq_len, width = gathered.shape
    hidden = gathered.astype(jnp.float32)
    normed = (
        hidden * lax.rsqrt(jnp.mean(hidden * hidden, axis=-1, keepdims=True) + 1e-06) * norm_gain
    ).astype(jnp.bfloat16)
    normed_flat = normed.reshape(dialogs * seq_len, width)
    query_cols = w_query.shape[1]
    keyval_cols = w_keyval.shape[2]
    pieces = (
        lax.all_gather(w_query, "dp", axis=0, tiled=True),
        lax.all_gather(w_keyval, "dp", axis=0, tiled=True),
    )
    keyval_piece = pieces[1].reshape(pieces[1].shape[0], 2 * keyval_cols)
    query_sum = jnp.dot(normed_flat, pieces[0], preferred_element_type=jnp.float32)
    keyval_sum = jnp.dot(normed_flat, keyval_piece, preferred_element_type=jnp.float32)
    positions = jnp.arange(seq_len)
    local_heads = query_cols // HEAD_DIM
    local_kv = keyval_cols // HEAD_DIM
    query = jax.vmap(lambda block: rotate(block, positions))(
        query_sum.reshape(dialogs, seq_len, local_heads, HEAD_DIM)
    ).astype(jnp.bfloat16)
    keys = jax.vmap(lambda block: rotate(block, positions))(
        keyval_sum[:, :keyval_cols].reshape(dialogs, seq_len, local_kv, HEAD_DIM)
    ).astype(jnp.bfloat16)
    values = (
        keyval_sum[:, keyval_cols:]
        .reshape(dialogs, seq_len, local_kv, HEAD_DIM)
        .astype(jnp.bfloat16)
    )
    pooled_context = jax.vmap(attend)(query, keys, values, lengths).astype(jnp.bfloat16)
    valid = (positions[None, :] < lengths[:, None]).astype(jnp.float32)
    pooled_input = (
        jnp.sum(hidden * valid[:, :, None], axis=1) / lengths.astype(jnp.float32)[:, None]
    )
    partial_out = jnp.dot(
        pooled_context,
        lax.all_gather(w_out, "dp", axis=1, tiled=True),
        preferred_element_type=jnp.float32,
    )
    projected = lax.psum(partial_out.astype(jnp.bfloat16), "mp").astype(jnp.float32)
    embedding = pooled_input + projected
    unit = embedding * lax.rsqrt(jnp.sum(embedding * embedding, axis=-1, keepdims=True) + 1e-06)
    unit = (unit * flags.astype(jnp.float32)[:, None]).astype(jnp.bfloat16)
    my_index = lax.axis_index("dp")
    owner_count = lax.axis_size("dp")
    my_count = jnp.sum(jnp.where(owner == my_index, counts, 0))
    members = residents[0]
    member_count = members.shape[0]
    inverse_norm = lax.rsqrt(
        jnp.einsum("md,md->m", members, members, preferred_element_type=jnp.float32) + 1e-06
    )
    member_start = lax.axis_index("mp") * member_count
    live = member_start + jnp.arange(member_count) < my_count
    table_size = owner.shape[0]
    cluster_ids = cluster[:, 0]
    destination = jnp.sum(
        jnp.where(jnp.arange(table_size)[None, :] == cluster_ids[:, None], owner[None, :], 0),
        axis=1,
    )
    capacity = max(1, -(-dialogs // owner_count))
    order = jnp.arange(dialogs)
    earlier = (destination[None, :] == destination[:, None]) & (order[None, :] < order[:, None])
    rank = jnp.sum(earlier.astype(jnp.int32), axis=1)
    onehot = (jnp.arange(owner_count)[:, None, None] == destination[None, None, :]) & (
        jnp.arange(capacity)[None, :, None] == rank[None, None, :]
    )
    outgoing = jnp.einsum(
        "ocn,nd->ocd", onehot.astype(jnp.bfloat16), unit, preferred_element_type=jnp.float32
    ).astype(jnp.bfloat16)
    query_rows = lax.all_to_all(outgoing, "dp", split_axis=0, concat_axis=0, tiled=True)
    dots = lax.dot_general(
        query_rows,
        members,
        (((query_rows.ndim - 1,), (1,)), ((), ())),
        preferred_element_type=jnp.float32,
    )
    returned = lax.all_to_all(
        jnp.where(live, logit_scale * dots * inverse_norm, 0.0).astype(jnp.bfloat16),
        "dp",
        split_axis=0,
        concat_axis=0,
        tiled=True,
    ).astype(jnp.float32)
    similarity = jnp.einsum(
        "ocn,ocm->nm", onehot.astype(jnp.float32), returned, precision=lax.Precision.HIGHEST
    )
    return similarity


def solution(mesh):
    in_specs = (
        P("dp", None, "mp"),
        P(),
        P("dp", "mp"),
        P("dp", None, "mp"),
        P("mp", "dp"),
        P("dp", "mp", None),
        P("dp"),
        P("dp", None),
        P(),
        P(),
        P("dp"),
    )
    out_specs = P("dp", "mp")
    return jax.shard_map(local, mesh=mesh, in_specs=in_specs, out_specs=out_specs, check_vma=False)
```

profile of v0, /device:TPU:0, one launch (start us, length us, event | category | flops | bytes accessed | tf_op | source)
XLA Modules:
  0.0 408.5 jit_solution(2310838354348667568)
XLA Ops:
  6.5 0.0 all-gather.9.cloned.1.call-start
  6.5 0.7 all-gather.9.cloned.1.call-update
  7.3 0.0 all-gather.5.cloned.1.call-start
  7.3 0.7 all-gather.5.cloned.1.call-update
  8.0 0.0 all-gather.7.cloned.1.call-start
  8.1 0.7 all-gather.7.cloned.1.call-update
  8.7 0.0 all-gather.11.cloned.1.call-start
  8.8 0.5 all-gather.11.cloned.1.call-update
  9.3 0.0 all-reduce.2.cloned.1.call-start
  9.4 0.7 convert_element_type.91
  10.0 0.7 convert_element_type.99
  10.7 0.8 select_reduce_fusion
  11.5 0.2 convert_reduce_fusion
  11.7 0.7 iota_compare_fusion.1
  12.4 0.2 multiply_cosine_fusion
  12.6 0.3 broadcast_and_fusion
  12.9 2.8 fusion.6
  15.7 97.3 %all-gather.9.cloned.1.call-done = bf16[3584,896]{1,0:T(8,128)(2,1)} async-done(((bf16[448,896]{1,0:T(8,128)(2,1)}), bf16[3584,896]{1,0:T(8,128)(2,1)}) %all-gather.9.cloned.1.call-update) | async-done | bytes 6422544 | tf_op jit(solution)/shard_map/all_gather | solution.py:59
  113.0 9.7 %copy.20 = bf16[896,3584]{1,0:T(8,128)(2,1)} copy(bf16[896,3584]{0,1:T(8,128)(2,1)} %bitcast.86) | data formatting | bytes 12845056 | tf_op jit(solution)/shard_map/dot_general | solution.py:63
  122.7 63.2 %all-gather.5.cloned.1.call-done = bf16[32,48,3584]{2,1,0:T(8,128)(2,1)} async-done(((bf16[32,48,896]{2,1,0:T(8,128)(2,1)}), bf16[32,48,3584]{2,1,0:T(8,128)(2,1)}) %all-gather.5.cloned.1.call-update) | async-done | bytes 11010064 | tf_op jit(solution)/shard_map/all_gather | solution.py:49
  185.8 0.0 copy-start.1
  185.8 8.9 %fusion = (f32[32,3584]{1,0:T(8,128)S(1)}, f32[32,48]{1,0:T(8,128)S(1)}) fusion(bf16[32,48,3584]{2,1,0:T(8,128)(2,1)} %all-gather.5.cloned.1.call-done, f32[32,48]{1,0:T(8,128)S(1)} %get-tuple-element.14), kind=kLoop, calls=%fused_computation.3 | loop fusion | flops 27408896 | bytes 11481088 | tf_op jit(solution)/shard_map/reduce_sum | solution.py:82
  194.8 0.0 copy-done.1
  194.8 0.0 slice-start
  194.8 11.0 %fusion.3 = bf16[32,48,3584]{2,1,0:T(8,128)(2,1)} fusion(bf16[32,48,3584]{2,1,0:T(8,128)(2,1)} %all-gather.5.cloned.1.call-done, f32[3584]{0:T(1024)S(1)} %copy-done.1, f32[32,48]{1,0:T(8,128)S(1)} %add_rsqrt_fusion), kind=kLoop, calls=%fused_computation.6 | loop fusion | flops 22020096 | bytes 22040576 | tf_op jit(solution)/shard_map/convert_element_type | solution.py:54
  205.7 28.8 %all-gather.7.cloned.1.call-done = bf16[3584,2,128]{2,1,0:T(2,128)(2,1)} async-done(((bf16[448,2,128]{2,1,0:T(2,128)(2,1)}), bf16[3584,2,128]{2,1,0:T(2,128)(2,1)}) %all-gather.7.cloned.1.call-update) | async-done | bytes 1835024 | tf_op jit(solution)/shard_map/all_gather | solution.py:60
  234.5 0.0 copy-start
  234.5 0.0 slice-start.1
  234.5 7.2 %fusion.22 = f32[1536,256]{1,0:T(8,128)S(1)} fusion(bf16[1536,3584]{1,0:T(8,128)(2,1)} %bitcast.84, bf16[448,8,2,128]{3,2,1,0:T(2,128)(2,1)} %bitcast.92), kind=kOutput, calls=%fused_computation.34 | convolution fusion | flops 2818572288 | bytes 14417920 | tf_op jit(solution)/shard_map/dot_general | solution.py:64
  241.7 0.1 slice.26
  241.8 0.1 slice.48
  241.8 0.3 fusion.36
  242.2 0.0 slice-done
  242.2 0.2 copy-done
  242.4 1.5 slice-done.1
  243.8 11.6 %fusion.4 = f32[32,48,7,128]{3,1,2,0:T(8,128)S(1)} fusion(bf16[7,128,3584,1]{2,1,0,3:T(8,128)(2,1)S(1)} %bitcast.89, bf16[32,48,3584]{2,1,0:T(8,128)(2,1)S(1)} %copy-done), kind=kOutput, calls=%fused_computation.7 | convolution fusion | flops 9865003008 | bytes 22937600 | tf_op jit(solution)/shard_map/dot_general | solution.py:63
  255.5 1.9 subtract_convert_fusion
  257.4 3.6 fusion.9
  261.0 2.1 fusion.8
  263.2 2.3 fusion.7
  265.5 0.0 copy-start.2
  265.5 0.0 copy-start.3
  265.5 70.8 %all-gather.11.cloned.1.call-done = bf16[896,3584]{0,1:T(8,128)(2,1)} async-done(((bf16[896,448]{0,1:T(8,128)(2,1)}), bf16[896,3584]{0,1:T(8,128)(2,1)}) %all-gather.11.cloned.1.call-update) | async-done | bytes 6422544 | tf_op jit(solution)/shard_map/all_gather | solution.py:86
  336.3 5.5 %convolution_convert_fusion.1 = bf16[32,3584]{1,0:T(8,128)(2,1)} fusion(bf16[896,3584]{0,1:T(8,128)(2,1)} %all-gather.11.cloned.1.call-done, f32[4,8,7,128]{3,2,1,0:T(8,128)S(1)} %bitcast.91, f32[32]{0:T(128)S(1)} %convert_element_type.91), kind=kOutput, calls=%fused_computation.20 | convolution fusion | flops 205692928 | bytes 6766720 | tf_op jit(solution)/shard_map/dot_general | solution.py:84
  341.8 0.0 all-reduce.2.cloned.1.call-update
  341.8 30.2 %all-reduce.2.cloned.1.call-done = bf16[32,3584]{1,0:T(8,128)(2,1)} async-done(((bf16[32,3584]{1,0:T(8,128)(2,1)}), bf16[32,3584]{1,0:T(8,128)(2,1)}) %all-reduce.2.cloned.1.call-update) | async-done | bytes 229392 | tf_op jit(solution)/shard_map/psum | solution.py:89
  372.0 1.2 multiply_reduce_fusion
  373.2 1.9 convolution_convert_fusion
  375.1 5.5 %all-to-all-start = ((bf16[8,4,3584]{2,1,0:T(4,128)(2,1)}), bf16[8,4,3584]{2,1,0:T(4,128)(2,1)S(1)}, u32[]{:S(2)}, u32[]{:S(2)}) async-start(bf16[8,4,3584]{2,1,0:T(4,128)(2,1)} %convolution_convert_fusion), calls=%async_computation | async-start | bytes 458752 | tf_op jit(solution)/shard_map/all_to_all | solution.py:119
  380.7 0.0 copy-done.2
  380.7 0.0 copy-done.3
  380.7 0.6 fusion.50
  381.3 0.7 add_compare_fusion
  382.0 6.7 %all-to-all-done = bf16[8,4,3584]{2,1,0:T(4,128)(2,1)S(1)} async-done(((bf16[8,4,3584]{2,1,0:T(4,128)(2,1)}), bf16[8,4,3584]{2,1,0:T(4,128)(2,1)S(1)}, u32[]{:S(2)}, u32[]{:S(2)}) %all-to-all-start) | async-done | bytes 229408 | tf_op jit(solution)/shard_map/all_to_all | solution.py:119
  388.7 3.2 fusion.33
  391.9 9.2 %all_to_all.10 = bf16[8,4,512]{2,1,0:T(4,128)(2,1)S(1)} all-to-all(bf16[8,4,512]{2,1,0:T(4,128)(2,1)S(1)} %fusion.33), channel_id=1, replica_groups=mesh['dp'=8,'mp'=4] {'dp'}, dimensions={0} | all-to-all | bytes 65536 | tf_op jit(solution)/shard_map/all_to_all | solution.py:126
  401.2 0.8 convolution_bitcast_fusion
  (10 shorter events, 0.1 us)
Async XLA Ops:
  6.5 106.4 %all-gather.9.cloned.1.call-start = ((), (), s32[]{:S(2)}) async-start(), calls=%async_computation.4 | async-start | bytes 7225344 | tf_op jit(solution)/shard_map/all_gather | solution.py:59
  7.3 178.6 %all-gather.5.cloned.1.call-start = ((), (), s32[]{:S(2)}) async-start(), calls=%async_computation.2 | async-start | bytes 13762560 | tf_op jit(solution)/shard_map/all_gather | solution.py:49
  8.0 226.5 %all-gather.7.cloned.1.call-start = ((), (), s32[]{:S(2)}) async-start(), calls=%async_computation.3 | async-start | bytes 2064384 | tf_op jit(solution)/shard_map/all_gather | solution.py:60
  8.7 327.5 %all-gather.11.cloned.1.call-start = ((), (), s32[]{:S(2)}) async-start(), calls=%async_computation.5 | async-start | bytes 7225344 | tf_op jit(solution)/shard_map/all_gather | solution.py:86
  9.3 362.7 %all-reduce.2.cloned.1.call-start = ((), (), s32[]{:S(2)}) async-start(), calls=%async_computation.6 | async-start | bytes 458752 | tf_op jit(solution)/shard_map/psum | solution.py:89
  185.8 8.9 %copy-start.1 = (f32[3584]{0:T(1024)S(1)}, f32[3584]{0:T(1024)}, u32[]{:S(2)}) copy-start(f32[3584]{0:T(1024)} %param.12) | copy-start | bytes 43012
  194.8 47.4 %slice-start = ((s8[6422528]{0:T(1024)(128)(4,1)}), s8[2228224]{0:T(1024)(128)(4,1)S(1)}, s32[]{:S(2)}) async-start(s8[6422528]{0:T(1024)(128)(4,1)} %bitcast.87), calls=%async_computation.7 | async-start | bytes 4456448
  234.5 7.8 %copy-start = (bf16[32,48,3584]{2,1,0:T(8,128)(2,1)S(1)}, bf16[32,48,3584]{2,1,0:T(8,128)(2,1)}, u32[]{:S(2)}) copy-start(bf16[32,48,3584]{2,1,0:T(8,128)(2,1)} %fusion.3) | copy-start | bytes 33030148
  234.5 9.3 %slice-start.1 = ((s8[6422528]{0:T(1024)(128)(4,1)}), s8[4194304]{0:T(1024)(128)(4,1)S(1)}, s32[]{:S(2)}) async-start(s8[6422528]{0:T(1024)(128)(4,1)} %bitcast.87), calls=%async_computation.8 | async-start | bytes 8388608
  265.5 115.2 %copy-start.2 = (s32[8]{0:T(128)S(1)}, s32[8]{0:T(128)}, u32[]{:S(2)}) copy-start(s32[8]{0:T(128)} %param.19) | copy-start | bytes 100
  265.5 115.2 %copy-start.3 = (s32[8]{0:T(128)S(1)}, s32[8]{0:T(128)}, u32[]{:S(2)}) copy-start(s32[8]{0:T(128)} %param.20) | copy-start | bytes 100
  375.1 13.5 %all-to-all-start = ((bf16[8,4,3584]{2,1,0:T(4,128)(2,1)}), bf16[8,4,3584]{2,1,0:T(4,128)(2,1)S(1)}, u32[]{:S(2)}, u32[]{:S(2)}) async-start(bf16[8,4,3584]{2,1,0:T(4,128)(2,1)} %convolution_convert_fusion), calls=%async_computation | async-start | bytes 458752 | tf_op jit(solution)/shard_map/all_to_all | solution.py:119
Sparse Core Ops, SparseCore 0:
  9.5 103.3 all-gather.8
  114.5 71.2 all-gather.4
  188.0 46.4 all-gather.6
  236.6 99.6 all-gather.10
  341.9 30.0 all-reduce.1
where the time goes:
time: 409 us
  waiting for transfers between devices  299 us (73%)
  matrix products  36.3 us (9%)
  other arithmetic  33 us (8%)
  between operations  13.3 us (3%)
  local copies, waits for them, and re-layouts  11.5 us (3%)
  blocking collectives  9.24 us (2%)
  starting transfers between devices  5.66 us (1%)
    all_gather x1, waiting for transfers between devices, local(): lax.all_gather(w_query, 'dp', axis=0, tiled=True)  97.3 us
    all_gather x1, waiting for transfers between devices, local(): lax.all_gather(w_out, 'dp', axis=1, tiled=True)  70.8 us
    all_gather x1, waiting for transfers between devices, local(): gathered = lax.all_gather(tokens, 'mp', axis=2, tiled=True)  63.2 us
    psum x1, waiting for transfers between devices, local(): lax.psum(partial_out.astype(jnp.bfloat16), 'mp').astype(jnp.float32)  30.2 us
    all_gather x1, waiting for transfers between devices, local(): lax.all_gather(w_keyval, 'dp', axis=0, tiled=True)  28.8 us
    dot_general x1, matrix products, local(): jnp.dot(normed_flat, pieces[0], preferred_element_type=jnp.float32)  11.6 us
    convert_element_type x1, other arithmetic, local(): normed = (hidden * lax.rsqrt(jnp.mean(hidden * hidden, axis=-1, keepdims=...  11 us
    dot_general x1, local copies, waits for them, and re-layouts, local(): jnp.dot(normed_flat, pieces[0], preferred_element_type=jnp.float32)  9.72 us
  transfers between devices with their start and end apart: 6, of which 6 were waited for; matrix products, arithmetic and copies ran while one was open for 16% of the time, Pallas kernels for 0%

commit v1 on v0

--- a/solution.py
+++ b/solution.py
@@ -7,6 +7,23 @@
 HEAD_DIM = 128
 rope_base = 1000000.0
 logit_scale = 100.0
+
+
+def view_enter(in_array, which_dim):
+    u_next = list(in_array.shape[1:])
+    u_next[which_dim] *= in_array.shape[0]
+    return jnp.moveaxis(in_array, 0, which_dim).reshape(u_next)
+
+
+def enter_the_tracks(u_in, dev_axis, row_dim):
+    n_shards = jax.lax.psum(1, dev_axis)
+    row_list = [(jj, (jj + 1) % n_shards) for jj in range(n_shards)]
+    crops = [u_in]
+    while len(crops) < n_shards:
+        crops.append(jax.lax.ppermute(crops[-1], dev_axis, row_list))
+    v_now = jax.lax.axis_index(dev_axis)
+    crops = jnp.stack(crops, axis=0)[(v_now - jnp.arange(n_shards)) % n_shards]
+    return view_enter(crops, row_dim)
 
 
 def rotate(values, positions):
@@ -57,7 +74,7 @@
     keyval_cols = w_keyval.shape[2]
     pieces = (
         lax.all_gather(w_query, "dp", axis=0, tiled=True),
-        lax.all_gather(w_keyval, "dp", axis=0, tiled=True),
+        enter_the_tracks(w_keyval, "dp", 0),
     )
     keyval_piece = pieces[1].reshape(pieces[1].shape[0], 2 * keyval_cols)
     query_sum = jnp.dot(normed_flat, pieces[0], preferred_element_type=jnp.float32)

time: 409 us -> 386 us (0.944)
  waiting for transfers between devices: 299 us -> 274 us
  local copies, waits for them, and re-layouts: 11.5 us -> 17.5 us
  matrix products: 36.3 us -> 31.9 us
    ppermute x0 -> x7, waiting for transfers between devices: none -> 81.6 us  [enter_the_tracks(): crops.append(jax.lax.ppermute(crops[-1], dev_axis, row_list))]
    all_gather x1, waiting for transfers between devices: 97.3 us -> 27.3 us  [local(): lax.all_gather(w_query, 'dp', axis=0, tiled=True)]
    all_gather x1 -> x0, waiting for transfers between devices: 28.8 us -> none  [local(): lax.all_gather(w_keyval, 'dp', axis=0, tiled=True)]
    all_gather x1, waiting for transfers between devices: 70.8 us -> 60.3 us  [local(): lax.all_gather(w_out, 'dp', axis=1, tiled=True)]
    gather x0 -> x1, local copies, waits for them, and re-layouts: none -> 5.35 us  [enter_the_tracks(): crops = jnp.stack(crops, axis=0)[(v_now - jnp.arange(n_shards)) % n_shards]]
    dot_general x1, matrix products: 7.17 us -> 3.03 us  [local(): jnp.dot(normed_flat, keyval_piece, preferred_element_type=jnp.float32)]
  transfers between devices with their start and end apart: 6 -> 12, of which waited for: 6 -> 12; matrix products, arithmetic and copies ran while one was open for 16% -> 17% of each run, Pallas kernels for 0% -> 0%
where the time goes in v1:
time: 386 us
  waiting for transfers between devices  274 us (71%)
  matrix products  31.9 us (8%)
  other arithmetic  30.7 us (8%)
  local copies, waits for them, and re-layouts  17.5 us (5%)
  between operations  13.4 us (3%)
  blocking collectives  9.24 us (2%)
  starting transfers between devices  8.94 us (2%)
    ppermute x7, waiting for transfers between devices, enter_the_tracks(): crops.append(jax.lax.ppermute(crops[-1], dev_axis, row_list))  81.6 us
    all_gather x1, waiting for transfers between devices, local(): gathered = lax.all_gather(tokens, 'mp', axis=2, tiled=True)  66.5 us
    all_gather x1, waiting for transfers between devices, local(): lax.all_gather(w_out, 'dp', axis=1, tiled=True)  60.3 us
    psum x1, waiting for transfers between devices, local(): lax.psum(partial_out.astype(jnp.bfloat16), 'mp').astype(jnp.float32)  30.2 us
    all_gather x1, waiting for transfers between devices, local(): lax.all_gather(w_query, 'dp', axis=0, tiled=True)  27.3 us
    dot_general x1, matrix products, local(): jnp.dot(normed_flat, pieces[0], preferred_element_type=jnp.float32)  11.6 us
    dot_general x1, local copies, waits for them, and re-layouts, local(): jnp.dot(normed_flat, pieces[0], preferred_element_type=jnp.float32)  9.54 us
    all_to_all x1, blocking collectives, local(): lax.all_to_all(jnp.where(live, logit_scale * dots * inverse_norm, 0.0).as...  9.24 us
  transfers between devices with their start and end apart: 12, of which 12 were waited for; matrix products, arithmetic and copies ran while one was open for 17% of the time, Pallas kernels for 0%

profile of v1, /device:TPU:0, one launch (start us, length us, event | category | flops | bytes accessed | tf_op | source)
XLA Modules:
  0.0 385.7 jit_solution(2076663594826325143)
XLA Ops:
  6.5 0.7 all-gather.6.cloned.1.call-update
  7.3 0.0 all-gather.4.cloned.1.call-start
  7.3 0.7 all-gather.4.cloned.1.call-update
  8.0 0.0 all-gather.8.cloned.1.call-start
  8.1 3.0 collective-permute-start
  11.0 0.0 all-gather.8.cloned.1.call-update
  11.1 0.0 all-reduce.2.cloned.1.call-start
  11.1 1.1 bitcast_dynamic-update-slice_fusion.7
  12.3 0.7 iota_compare_fusion.1
  13.0 0.7 convert_element_type.91
  13.7 0.8 select_reduce_fusion
  14.4 0.2 convert_reduce_fusion
  14.6 0.7 convert_element_type.99
  15.3 2.8 fusion.6
  18.1 0.2 multiply_cosine_fusion
  18.3 0.3 broadcast_and_fusion
  18.6 1.3 collective-permute-done
  19.9 0.3 collective-permute-start.1
  20.2 0.2 bitcast_dynamic-update-slice_fusion.6
  20.4 13.9 %collective-permute-done.1 = bf16[448,2,128]{2,1,0:T(2,128)(2,1)S(1)} collective-permute-done((bf16[448,2,128]{2,1,0:T(2,128)(2,1)S(1)}, bf16[448,2,128]{2,1,0:T(2,128)(2,1)S(1)}, u32[]{:S(2)}, u32[]{:S(2)}) %collective-permute-start.1) | collective-permute-done | bytes 229408 | tf_op jit(solution)/shard_map/ppermute | solution.py:23
  34.2 0.0 collective-permute-start.2
  34.2 0.2 bitcast_dynamic-update-slice_fusion.5
  34.4 14.1 %collective-permute-done.2 = bf16[448,2,128]{2,1,0:T(2,128)(2,1)S(1)} collective-permute-done((bf16[448,2,128]{2,1,0:T(2,128)(2,1)S(1)}, bf16[448,2,128]{2,1,0:T(2,128)(2,1)S(1)}, u32[]{:S(2)}, u32[]{:S(2)}) %collective-permute-start.2) | collective-permute-done | bytes 229408 | tf_op jit(solution)/shard_map/ppermute | solution.py:23
  48.5 0.2 bitcast_dynamic-update-slice_fusion.4
  48.7 14.1 %collective-permute-done.3 = bf16[448,2,128]{2,1,0:T(2,128)(2,1)S(1)} collective-permute-done((bf16[448,2,128]{2,1,0:T(2,128)(2,1)S(1)}, bf16[448,2,128]{2,1,0:T(2,128)(2,1)S(1)}, u32[]{:S(2)}, u32[]{:S(2)}) %collective-permute-start.3) | collective-permute-done | bytes 229408 | tf_op jit(solution)/shard_map/ppermute | solution.py:23
  62.8 0.2 bitcast_dynamic-update-slice_fusion.3
  63.0 8.5 %collective-permute-done.4 = bf16[448,2,128]{2,1,0:T(2,128)(2,1)S(1)} collective-permute-done((bf16[448,2,128]{2,1,0:T(2,128)(2,1)S(1)}, bf16[448,2,128]{2,1,0:T(2,128)(2,1)S(1)}, u32[]{:S(2)}, u32[]{:S(2)}) %collective-permute-start.4) | collective-permute-done | bytes 229408 | tf_op jit(solution)/shard_map/ppermute | solution.py:23
  71.5 0.0 collective-permute-start.5
  71.5 0.2 bitcast_dynamic-update-slice_fusion.2
  71.7 15.0 %collective-permute-done.5 = bf16[448,2,128]{2,1,0:T(2,128)(2,1)S(1)} collective-permute-done((bf16[448,2,128]{2,1,0:T(2,128)(2,1)S(1)}, bf16[448,2,128]{2,1,0:T(2,128)(2,1)S(1)}, u32[]{:S(2)}, u32[]{:S(2)}) %collective-permute-start.5) | collective-permute-done | bytes 229408 | tf_op jit(solution)/shard_map/ppermute | solution.py:23
  86.7 0.0 collective-permute-start.6
  86.7 0.2 bitcast_dynamic-update-slice_fusion.1
  86.9 14.7 %collective-permute-done.6 = bf16[448,2,128]{2,1,0:T(2,128)(2,1)S(1)} collective-permute-done((bf16[448,2,128]{2,1,0:T(2,128)(2,1)S(1)}, bf16[448,2,128]{2,1,0:T(2,128)(2,1)S(1)}, u32[]{:S(2)}, u32[]{:S(2)}) %collective-permute-start.6) | collective-permute-done | bytes 229408 | tf_op jit(solution)/shard_map/ppermute | solution.py:23
  101.7 0.2 bitcast_dynamic-update-slice_fusion
  101.9 5.3 %gather_fusion = bf16[8,448,2,128]{3,2,1,0:T(2,128)(2,1)} fusion(bf16[8,448,2,128]{3,2,1,0:T(2,128)(2,1)S(1)} %bitcast_dynamic-update-slice_fusion, s32[1024]{0:T(1024)S(1)} %pad_clamp_fusion), kind=kCustom, calls=%fused_computation | custom fusion | bytes 3670048 | tf_op jit(solution)/shard_map/gather | solution.py:25
  107.2 27.3 %all-gather.6.cloned.1.call-done = bf16[3584,896]{1,0:T(8,128)(2,1)} async-done(((bf16[448,896]{1,0:T(8,128)(2,1)}), bf16[3584,896]{1,0:T(8,128)(2,1)}) %all-gather.6.cloned.1.call-update) | async-done | bytes 6422544 | tf_op jit(solution)/shard_map/all_gather | solution.py:76
  134.5 9.5 %copy.20 = bf16[896,3584]{1,0:T(8,128)(2,1)} copy(bf16[896,3584]{0,1:T(8,128)(2,1)} %bitcast.105) | data formatting | bytes 12845056 | tf_op jit(solution)/shard_map/dot_general | solution.py:80
  144.1 66.5 %all-gather.4.cloned.1.call-done = bf16[32,48,3584]{2,1,0:T(8,128)(2,1)} async-done(((bf16[32,48,896]{2,1,0:T(8,128)(2,1)}), bf16[32,48,3584]{2,1,0:T(8,128)(2,1)}) %all-gather.4.cloned.1.call-update) | async-done | bytes 11010064 | tf_op jit(solution)/shard_map/all_gather | solution.py:66
  210.6 8.9 %fusion = (f32[32,3584]{1,0:T(8,128)S(1)}, f32[32,48]{1,0:T(8,128)S(1)}) fusion(bf16[32,48,3584]{2,1,0:T(8,128)(2,1)} %all-gather.4.cloned.1.call-done, f32[32,48]{1,0:T(8,128)S(1)} %get-tuple-element.14), kind=kLoop, calls=%fused_computation.4 | loop fusion | flops 27408896 | bytes 11481088 | tf_op jit(solution)/shard_map/reduce_sum | solution.py:99
  219.5 8.4 %fusion.3 = bf16[32,48,3584]{2,1,0:T(8,128)(2,1)S(1)} fusion(bf16[32,48,3584]{2,1,0:T(8,128)(2,1)} %all-gather.4.cloned.1.call-done, f32[3584]{0:T(1024)S(1)} %copy-done.1, f32[32,48]{1,0:T(8,128)S(1)} %add_rsqrt_fusion), kind=kLoop, calls=%fused_computation.7 | loop fusion | flops 22020096 | bytes 22040576 | tf_op jit(solution)/shard_map/convert_element_type | solution.py:71
  228.0 3.0 fusion.22
  231.0 0.1 slice.28
  231.0 0.1 slice.50
  231.1 0.3 fusion.36
  231.5 11.6 %fusion.4 = f32[32,48,7,128]{3,1,2,0:T(8,128)S(1)} fusion(bf16[7,128,3584,1]{2,1,0,3:T(8,128)(2,1)S(1)} %bitcast.108, bf16[32,48,3584]{2,1,0:T(8,128)(2,1)S(1)} %fusion.3), kind=kOutput, calls=%fused_computation.8 | convolution fusion | flops 9865003008 | bytes 22937600 | tf_op jit(solution)/shard_map/dot_general | solution.py:80
  243.1 2.2 subtract_convert_fusion
  245.3 3.4 fusion.9
  248.7 2.1 fusion.8
  250.8 2.3 fusion.7
  253.1 0.0 copy-start.2
  253.2 0.0 copy-start.3
  253.2 60.3 %all-gather.8.cloned.1.call-done = bf16[896,3584]{0,1:T(8,128)(2,1)} async-done(((bf16[896,448]{0,1:T(8,128)(2,1)}), bf16[896,3584]{0,1:T(8,128)(2,1)}) %all-gather.8.cloned.1.call-update) | async-done | bytes 6422544 | tf_op jit(solution)/shard_map/all_gather | solution.py:103
  313.4 5.5 %convolution_convert_fusion.1 = bf16[32,3584]{1,0:T(8,128)(2,1)} fusion(bf16[896,3584]{0,1:T(8,128)(2,1)} %all-gather.8.cloned.1.call-done, f32[4,8,7,128]{3,2,1,0:T(8,128)S(1)} %bitcast.111, f32[32]{0:T(128)S(1)} %convert_element_type.91), kind=kOutput, calls=%fused_computation.21 | convolution fusion | flops 205692928 | bytes 6766720 | tf_op jit(solution)/shard_map/dot_general | solution.py:101
  319.0 0.0 all-reduce.2.cloned.1.call-update
  319.0 30.2 %all-reduce.2.cloned.1.call-done = bf16[32,3584]{1,0:T(8,128)(2,1)} async-done(((bf16[32,3584]{1,0:T(8,128)(2,1)}), bf16[32,3584]{1,0:T(8,128)(2,1)}) %all-reduce.2.cloned.1.call-update) | async-done | bytes 229392 | tf_op jit(solution)/shard_map/psum | solution.py:106
  349.2 1.2 multiply_reduce_fusion
  350.4 1.9 convolution_convert_fusion
  352.4 5.5 %all-to-all-start = ((bf16[8,4,3584]{2,1,0:T(4,128)(2,1)}), bf16[8,4,3584]{2,1,0:T(4,128)(2,1)S(1)}, u32[]{:S(2)}, u32[]{:S(2)}) async-start(bf16[8,4,3584]{2,1,0:T(4,128)(2,1)} %convolution_convert_fusion), calls=%async_computation | async-start | bytes 458752 | tf_op jit(solution)/shard_map/all_to_all | solution.py:136
  357.9 0.6 fusion.50
  358.5 0.7 add_compare_fusion
  359.2 6.7 %all-to-all-done = bf16[8,4,3584]{2,1,0:T(4,128)(2,1)S(1)} async-done(((bf16[8,4,3584]{2,1,0:T(4,128)(2,1)}), bf16[8,4,3584]{2,1,0:T(4,128)(2,1)S(1)}, u32[]{:S(2)}, u32[]{:S(2)}) %all-to-all-start) | async-done | bytes 229408 | tf_op jit(solution)/shard_map/all_to_all | solution.py:136
  365.9 3.2 fusion.33
  369.1 9.2 %all_to_all.10 = bf16[8,4,512]{2,1,0:T(4,128)(2,1)S(1)} all-to-all(bf16[8,4,512]{2,1,0:T(4,128)(2,1)S(1)} %fusion.33), channel_id=1, replica_groups=mesh['dp'=8,'mp'=4] {'dp'}, dimensions={0} | all-to-all | bytes 65536 | tf_op jit(solution)/shard_map/all_to_all | solution.py:143
  378.4 0.8 convolution_bitcast_fusion
  (25 shorter events, 0.1 us)
Async XLA Ops:
  6.5 128.0 %all-gather.6.cloned.1.call-start = ((), (), s32[]{:S(2)}) async-start(), calls=%async_computation.3 | async-start | bytes 7225344 | tf_op jit(solution)/shard_map/all_gather | solution.py:76
  7.3 203.3 %all-gather.4.cloned.1.call-start = ((), (), s32[]{:S(2)}) async-start(), calls=%async_computation.2 | async-start | bytes 13762560 | tf_op jit(solution)/shard_map/all_gather | solution.py:66
  8.0 305.4 %all-gather.8.cloned.1.call-start = ((), (), s32[]{:S(2)}) async-start(), calls=%async_computation.4 | async-start | bytes 7225344 | tf_op jit(solution)/shard_map/all_gather | solution.py:103
  8.1 11.8 %collective-permute-start = (bf16[448,2,128]{2,1,0:T(2,128)(2,1)}, bf16[448,2,128]{2,1,0:T(2,128)(2,1)S(1)}, u32[]{:S(2)}, u32[]{:S(2)}) collective-permute-start(bf16[448,2,128]{2,1,0:T(2,128)(2,1)} %param.14), channel_id=1, source_target_pairs={{0,4},{4,8},{8,12},{12,16},{16,20},{20,24},{24,28},{28,0},{1,5},{5... | collective-permute-start | bytes 688136 | tf_op jit(solution)/shard_map/ppermute | solution.py:23
  11.1 338.1 %all-reduce.2.cloned.1.call-start = ((), (), s32[]{:S(2)}) async-start(), calls=%async_computation.5 | async-start | bytes 458752 | tf_op jit(solution)/shard_map/psum | solution.py:106
  19.9 14.3 %collective-permute-start.1 = (bf16[448,2,128]{2,1,0:T(2,128)(2,1)S(1)}, bf16[448,2,128]{2,1,0:T(2,128)(2,1)S(1)}, u32[]{:S(2)}, u32[]{:S(2)}) collective-permute-start(bf16[448,2,128]{2,1,0:T(2,128)(2,1)S(1)} %collective-permute-done), channel_id=1, source_target_pairs={{0,4},{4,8},{8,12},{12,16},{16,20},{20,24},{24,28},{28,0},{1,5},{5... | collective-permute-start | bytes 688136 | tf_op jit(solution)/shard_map/ppermute | solution.py:23
  34.2 14.3 %collective-permute-start.2 = (bf16[448,2,128]{2,1,0:T(2,128)(2,1)S(1)}, bf16[448,2,128]{2,1,0:T(2,128)(2,1)S(1)}, u32[]{:S(2)}, u32[]{:S(2)}) collective-permute-start(bf16[448,2,128]{2,1,0:T(2,128)(2,1)S(1)} %collective-permute-done.1), channel_id=1, source_target_pairs={{0,4},{4,8},{8,12},{12,16},{16,20},{20,24},{24,28},{28,0},{1,5},{5... | collective-permute-start | bytes 688136 | tf_op jit(solution)/shard_map/ppermute | solution.py:23
  48.5 14.3 %collective-permute-start.3 = (bf16[448,2,128]{2,1,0:T(2,128)(2,1)S(1)}, bf16[448,2,128]{2,1,0:T(2,128)(2,1)S(1)}, u32[]{:S(2)}, u32[]{:S(2)}) collective-permute-start(bf16[448,2,128]{2,1,0:T(2,128)(2,1)S(1)} %collective-permute-done.2), channel_id=1, source_target_pairs={{0,4},{4,8},{8,12},{12,16},{16,20},{20,24},{24,28},{28,0},{1,5},{5... | collective-permute-start | bytes 688136 | tf_op jit(solution)/shard_map/ppermute | solution.py:23
  62.8 8.7 %collective-permute-start.4 = (bf16[448,2,128]{2,1,0:T(2,128)(2,1)S(1)}, bf16[448,2,128]{2,1,0:T(2,128)(2,1)S(1)}, u32[]{:S(2)}, u32[]{:S(2)}) collective-permute-start(bf16[448,2,128]{2,1,0:T(2,128)(2,1)S(1)} %collective-permute-done.3), channel_id=1, source_target_pairs={{0,4},{4,8},{8,12},{12,16},{16,20},{20,24},{24,28},{28,0},{1,5},{5... | collective-permute-start | bytes 688136 | tf_op jit(solution)/shard_map/ppermute | solution.py:23
  71.5 15.2 %collective-permute-start.5 = (bf16[448,2,128]{2,1,0:T(2,128)(2,1)S(1)}, bf16[448,2,128]{2,1,0:T(2,128)(2,1)S(1)}, u32[]{:S(2)}, u32[]{:S(2)}) collective-permute-start(bf16[448,2,128]{2,1,0:T(2,128)(2,1)S(1)} %collective-permute-done.4), channel_id=1, source_target_pairs={{0,4},{4,8},{8,12},{12,16},{16,20},{20,24},{24,28},{28,0},{1,5},{5... | collective-permute-start | bytes 688136 | tf_op jit(solution)/shard_map/ppermute | solution.py:23
  86.7 14.9 %collective-permute-start.6 = (bf16[448,2,128]{2,1,0:T(2,128)(2,1)S(1)}, bf16[448,2,128]{2,1,0:T(2,128)(2,1)S(1)}, u32[]{:S(2)}, u32[]{:S(2)}) collective-permute-start(bf16[448,2,128]{2,1,0:T(2,128)(2,1)S(1)} %collective-permute-done.5), channel_id=1, source_target_pairs={{0,4},{4,8},{8,12},{12,16},{16,20},{20,24},{24,28},{28,0},{1,5},{5... | collective-permute-start | bytes 688136 | tf_op jit(solution)/shard_map/ppermute | solution.py:23
  210.6 8.9 %copy-start.1 = (f32[3584]{0:T(1024)S(1)}, f32[3584]{0:T(1024)}, u32[]{:S(2)}) copy-start(f32[3584]{0:T(1024)} %param.12) | copy-start | bytes 43012
  219.5 8.4 %copy-start = (bf16[8,448,2,128]{3,2,1,0:T(2,128)(2,1)S(1)}, bf16[8,448,2,128]{3,2,1,0:T(2,128)(2,1)}, u32[]{:S(2)}) copy-start(bf16[8,448,2,128]{3,2,1,0:T(2,128)(2,1)} %gather_fusion) | copy-start | bytes 5505028
  219.5 11.9 %slice-start = ((s8[6422528]{0:T(1024)(128)(4,1)}), s8[4194304]{0:T(1024)(128)(4,1)S(1)}, s32[]{:S(2)}) async-start(s8[6422528]{0:T(1024)(128)(4,1)} %bitcast.106), calls=%async_computation.6 | async-start | bytes 8388608
  227.9 3.5 slice-start.1
  253.1 104.7 %copy-start.2 = (s32[8]{0:T(128)S(1)}, s32[8]{0:T(128)}, u32[]{:S(2)}) copy-start(s32[8]{0:T(128)} %param.19) | copy-start | bytes 100
  253.2 104.7 %copy-start.3 = (s32[8]{0:T(128)S(1)}, s32[8]{0:T(128)}, u32[]{:S(2)}) copy-start(s32[8]{0:T(128)} %param.20) | copy-start | bytes 100
  352.4 13.5 %all-to-all-start = ((bf16[8,4,3584]{2,1,0:T(4,128)(2,1)}), bf16[8,4,3584]{2,1,0:T(4,128)(2,1)S(1)}, u32[]{:S(2)}, u32[]{:S(2)}) async-start(bf16[8,4,3584]{2,1,0:T(4,128)(2,1)} %convolution_convert_fusion), calls=%async_computation | async-start | bytes 458752 | tf_op jit(solution)/shard_map/all_to_all | solution.py:136
Sparse Core Ops, SparseCore 0:
  9.5 124.9 all-gather.5
  136.1 74.4 all-gather.3
  212.8 100.6 all-gather.7
  319.1 30.0 all-reduce.1
